TPU v7x, 512 devices: a whole 4x4x16 slice. The times are simulated.
512 devices in a mesh: gx: 8 (over y, core), gy: 16 (over z), gz: 4 (over x).
Axes of the slice: x: 4, y: 4, z: 16, core: 2. Of those that a mesh axis runs over, the one named last changes fastest.
Arguments:
- history: float32 [56, 32, 128, 1024], P(None, 'gz', 'gy', 'gx'), may hold values from -6 to 6
- start: float32 [4, 32, 128, 1024], P(None, 'gz', 'gy', 'gx'), may hold values from -51 to 51
- diagonal: float32 [32, 128, 1024], P('gz', 'gy', 'gx'), may hold values from 0.25 to 2
Outputs:
- new_basis: float32 [20, 32, 128, 1024], P(None, 'gz', 'gy', 'gx')
- r_factor: float32 [20, 20], replicated
All inputs are finite; a program needn't handle non-finite values.
Results may differ from a plain program's by a relative error of at most 0.0003.
Values sent between devices are 32-bit elements; how exact they have to be, the bound alone decides.
A program may use at most 64 MiB of HBM per device.

v0:
```python
import jax
import jax.numpy as jnp
from jax import lax
from jax.sharding import PartitionSpec as P

STEPS = 4
HIST = 56
COLS = 20


def with_halo(block, sides, width):
    for axis, dim in sides:
        count = lax.axis_size(axis)
        forward = [(i, i + 1) for i in range(count - 1)]
        backward = [(target, source) for source, target in forward]
        low = lax.ppermute(
            lax.slice_in_dim(block, block.shape[dim] - width, None, axis=dim), axis, forward
        )
        high = lax.ppermute(lax.slice_in_dim(block, 0, width, axis=dim), axis, backward)
        block = jnp.concatenate([low, block, high], axis=dim)
    return block


def crop_cells(array, margin):
    return array[
        ...,
        margin : array.shape[-3] - margin,
        margin : array.shape[-2] - margin,
        margin : array.shape[-1] - margin,
    ]


def scaled_from_padded(padded, diag_inner, mask_inner):
    center = crop_cells(padded, 1)
    beside = padded[:, 2:, 1:-1, 1:-1] + padded[:, :-2, 1:-1, 1:-1]
    beside = beside + padded[:, 1:-1, 2:, 1:-1] + padded[:, 1:-1, :-2, 1:-1]
    beside = beside + padded[:, 1:-1, 1:-1, 2:] + padded[:, 1:-1, 1:-1, :-2]
    return ((6.0 + diag_inner[None]) * center - beside - 7.0 * center) / 7.0 * mask_inner


def on_device(history, start, diagonal):
    depth_z, depth_y, depth_x = diagonal.shape

    def scaled_step(field):
        padded = with_halo(field, (("gx", 3), ("gy", 2), ("gz", 1)), 1)
        return scaled_from_padded(padded, diagonal, 1.0)

    blocks = [start, scaled_step(start)]
    for level in range(1, STEPS):
        blocks.append(2.0 * scaled_step(blocks[level]) - blocks[level - 1])
    basis = jnp.concatenate(blocks, axis=0)
    cell_total = float(
        depth_z
        * depth_y
        * depth_x
        * lax.axis_size("gx")
        * lax.axis_size("gy")
        * lax.axis_size("gz")
    )
    flat_basis = basis.reshape(COLS, -1)
    flat_hist = history.reshape(HIST, -1)
    highest = lax.Precision.HIGHEST
    local_coef = jnp.dot(
        flat_hist, flat_basis.T, precision=highest, preferred_element_type=jnp.float32
    )
    coef = lax.psum(local_coef, ("gx", "gy", "gz")) / cell_total
    projected = flat_basis - jnp.dot(
        coef.T, flat_hist, precision=highest, preferred_element_type=jnp.float32
    )
    local_gram = jnp.dot(
        projected, projected.T, precision=highest, preferred_element_type=jnp.float32
    )
    gram = lax.psum(local_gram, ("gx", "gy", "gz")) / cell_total
    lower = jnp.linalg.cholesky(gram)
    solved = lax.linalg.triangular_solve(lower, projected, left_side=True, lower=True)
    return (solved.reshape(basis.shape), lower.T)


def solution(mesh):
    return jax.shard_map(
        on_device,
        mesh=mesh,
        in_specs=(P(None, "gz", "gy", "gx"), P(None, "gz", "gy", "gx"), P("gz", "gy", "gx")),
        out_specs=(P(None, "gz", "gy", "gx"), P()),
        check_vma=False,
    )
```

profile of v0, /device:TPU:1, one launch (start us, length us, event | category | flops | bytes accessed | tf_op | source)
XLA Modules:
  0.0 336.8 jit_solution(8611840169034410942)
XLA Ops:
  0.6 1.1 fusion.57
  1.8 8.8 %collective-permute-start.1 = (f32[4,8,8,1]{3,2,1,0:T(8,128)S(1)}, f32[4,8,8,1]{3,2,1,0:T(8,128)S(1)}, u32[]{:S(2)}, u32[]{:S(2)}) collective-permute-start(f32[4,8,8,1]{3,2,1,0:T(8,128)S(1)} %get-tuple-element.32), channel_id=1, source_target_pairs={{64,0},{128,64},{192,128},{256,192},{320,256},{384,320},{448,384},... | collective-permute-start | bytes 3080 | tf_op jit(solution)/shard_map/ppermute | solution.py:19
  10.6 1.9 collective-permute-start
  12.5 1.9 collective-permute-done
  14.4 1.2 pad_maximum_fusion.101
  15.7 1.3 collective-permute-start.3
  17.0 4.0 %collective-permute-start.2 = (f32[4,8,1,130]{3,2,1,0:T(1,128)S(1)}, f32[4,8,1,130]{3,2,1,0:T(1,128)S(1)}, u32[]{:S(2)}, u32[]{:S(2)}) collective-permute-start(f32[4,8,1,130]{3,2,1,0:T(1,128)S(1)} %get-tuple-element.25), channel_id=1, source_target_pairs={{0,4},{4,8},{8,12},{12,16},{16,20},{20,24},{24,28},{28,32},{32,36}... | collective-permute-start | bytes 49928 | tf_op jit(solution)/shard_map/ppermute | solution.py:16
  21.0 1.0 collective-permute-done.2
  22.0 0.9 pad_maximum_fusion.91
  22.8 1.3 collective-permute-start.4
  24.1 4.0 %collective-permute-start.5 = (f32[4,1,10,130]{3,2,1,0:T(8,128)S(1)}, f32[4,1,10,130]{3,2,1,0:T(8,128)S(1)}, u32[]{:S(2)}, u32[]{:S(2)}) collective-permute-start(f32[4,1,10,130]{3,2,1,0:T(8,128)S(1)} %get-tuple-element.17), channel_id=1, source_target_pairs={{0,1},{1,2},{2,3},{4,5},{5,6},{6,7},{8,9},{9,10},{10,11},{12,13},{... | collective-permute-start | bytes 62408 | tf_op jit(solution)/shard_map/ppermute | solution.py:16
  28.1 0.8 broadcast_multiply_fusion.1
  28.9 0.5 collective-permute-done.5
  29.4 2.1 broadcast_multiply_fusion
  31.7 3.7 %collective-permute-start.7 = (f32[4,8,8,1]{3,2,1,0:T(8,128)S(1)}, f32[4,8,8,1]{3,2,1,0:T(8,128)S(1)}, u32[]{:S(2)}, u32[]{:S(2)}) collective-permute-start(f32[4,8,8,1]{3,2,1,0:T(8,128)S(1)} %get-tuple-element.30), channel_id=1, source_target_pairs={{64,0},{128,64},{192,128},{256,192},{320,256},{384,320},{448,384},... | collective-permute-start | bytes 3080 | tf_op jit(solution)/shard_map/ppermute | solution.py:19
  35.4 4.8 %collective-permute-start.6 = (f32[4,8,8,1]{3,2,1,0:T(8,128)S(1)}, f32[4,8,8,1]{3,2,1,0:T(8,128)S(1)}, u32[]{:S(2)}, u32[]{:S(2)}) collective-permute-start(f32[4,8,8,1]{3,2,1,0:T(8,128)S(1)} %get-tuple-element.31), channel_id=1, source_target_pairs={{0,64},{64,128},{128,192},{192,256},{256,320},{320,384},{384,448},... | collective-permute-start | bytes 3080 | tf_op jit(solution)/shard_map/ppermute | solution.py:16
  40.2 0.7 collective-permute-done.7
  40.9 1.2 collective-permute-done.6
  42.1 0.3 pad_maximum_fusion.98
  42.4 1.3 collective-permute-start.9
  43.7 4.6 %collective-permute-start.8 = (f32[4,8,1,130]{3,2,1,0:T(1,128)S(1)}, f32[4,8,1,130]{3,2,1,0:T(1,128)S(1)}, u32[]{:S(2)}, u32[]{:S(2)}) collective-permute-start(f32[4,8,1,130]{3,2,1,0:T(1,128)S(1)} %get-tuple-element.23), channel_id=1, source_target_pairs={{0,4},{4,8},{8,12},{12,16},{16,20},{20,24},{24,28},{28,32},{32,36}... | collective-permute-start | bytes 49928 | tf_op jit(solution)/shard_map/ppermute | solution.py:16
  48.3 1.0 collective-permute-done.8
  49.4 1.3 collective-permute-start.10
  50.7 4.6 %collective-permute-start.11 = (f32[4,1,10,130]{3,2,1,0:T(8,128)S(1)}, f32[4,1,10,130]{3,2,1,0:T(8,128)S(1)}, u32[]{:S(2)}, u32[]{:S(2)}) collective-permute-start(f32[4,1,10,130]{3,2,1,0:T(8,128)S(1)} %get-tuple-element.15), channel_id=1, source_target_pairs={{0,1},{1,2},{2,3},{4,5},{5,6},{6,7},{8,9},{9,10},{10,11},{12,13},{... | collective-permute-start | bytes 62408 | tf_op jit(solution)/shard_map/ppermute | solution.py:16
  55.4 1.3 collective-permute-done.11
  56.7 0.4 constant_dynamic-update-slice_fusion.1
  57.2 1.9 collective-permute-start.13
  59.1 6.1 %collective-permute-start.12 = (f32[4,8,8,1]{3,2,1,0:T(8,128)S(1)}, f32[4,8,8,1]{3,2,1,0:T(8,128)S(1)}, u32[]{:S(2)}, u32[]{:S(2)}) collective-permute-start(f32[4,8,8,1]{3,2,1,0:T(8,128)S(1)} %get-tuple-element.29), channel_id=1, source_target_pairs={{0,64},{64,128},{128,192},{192,256},{256,320},{320,384},{384,448},... | collective-permute-start | bytes 3080 | tf_op jit(solution)/shard_map/ppermute | solution.py:16
  65.2 0.7 collective-permute-done.13
  65.9 1.2 collective-permute-done.12
  67.1 0.3 pad_maximum_fusion.95
  67.4 1.3 collective-permute-start.15
  68.7 4.6 %collective-permute-start.14 = (f32[4,8,1,130]{3,2,1,0:T(1,128)S(1)}, f32[4,8,1,130]{3,2,1,0:T(1,128)S(1)}, u32[]{:S(2)}, u32[]{:S(2)}) collective-permute-start(f32[4,8,1,130]{3,2,1,0:T(1,128)S(1)} %get-tuple-element.21), channel_id=1, source_target_pairs={{0,4},{4,8},{8,12},{12,16},{16,20},{20,24},{24,28},{28,32},{32,36}... | collective-permute-start | bytes 49928 | tf_op jit(solution)/shard_map/ppermute | solution.py:16
  73.3 1.0 collective-permute-done.14
  74.4 1.4 collective-permute-start.16
  75.8 4.6 %collective-permute-start.17 = (f32[4,1,10,130]{3,2,1,0:T(8,128)S(1)}, f32[4,1,10,130]{3,2,1,0:T(8,128)S(1)}, u32[]{:S(2)}, u32[]{:S(2)}) collective-permute-start(f32[4,1,10,130]{3,2,1,0:T(8,128)S(1)} %get-tuple-element.13), channel_id=1, source_target_pairs={{0,1},{1,2},{2,3},{4,5},{5,6},{6,7},{8,9},{9,10},{10,11},{12,13},{... | collective-permute-start | bytes 62408 | tf_op jit(solution)/shard_map/ppermute | solution.py:16
  80.5 1.3 collective-permute-done.17
  81.8 0.4 constant_dynamic-update-slice_fusion
  82.3 1.9 collective-permute-start.19
  84.3 6.1 %collective-permute-start.18 = (f32[4,8,8,1]{3,2,1,0:T(8,128)S(1)}, f32[4,8,8,1]{3,2,1,0:T(8,128)S(1)}, u32[]{:S(2)}, u32[]{:S(2)}) collective-permute-start(f32[4,8,8,1]{3,2,1,0:T(8,128)S(1)} %get-tuple-element.27), channel_id=1, source_target_pairs={{0,64},{64,128},{128,192},{192,256},{256,320},{320,384},{384,448},... | collective-permute-start | bytes 3080 | tf_op jit(solution)/shard_map/ppermute | solution.py:16
  90.3 0.7 collective-permute-done.19
  91.0 1.2 collective-permute-done.18
  92.2 0.3 pad_maximum_fusion.92
  92.5 1.3 collective-permute-start.21
  93.8 4.6 %collective-permute-start.20 = (f32[4,8,1,130]{3,2,1,0:T(1,128)S(1)}, f32[4,8,1,130]{3,2,1,0:T(1,128)S(1)}, u32[]{:S(2)}, u32[]{:S(2)}) collective-permute-start(f32[4,8,1,130]{3,2,1,0:T(1,128)S(1)} %get-tuple-element.19), channel_id=1, source_target_pairs={{0,4},{4,8},{8,12},{12,16},{16,20},{20,24},{24,28},{28,32},{32,36}... | collective-permute-start | bytes 49928 | tf_op jit(solution)/shard_map/ppermute | solution.py:16
  98.4 1.0 collective-permute-done.20
  99.5 1.3 collective-permute-start.22
  100.8 4.6 %collective-permute-start.23 = (f32[4,1,10,130]{3,2,1,0:T(8,128)S(1)}, f32[4,1,10,130]{3,2,1,0:T(8,128)S(1)}, u32[]{:S(2)}, u32[]{:S(2)}) collective-permute-start(f32[4,1,10,130]{3,2,1,0:T(8,128)S(1)} %get-tuple-element.11), channel_id=1, source_target_pairs={{0,1},{1,2},{2,3},{4,5},{5,6},{6,7},{8,9},{9,10},{10,11},{12,13},{... | collective-permute-start | bytes 62408 | tf_op jit(solution)/shard_map/ppermute | solution.py:16
  105.5 1.3 collective-permute-done.23
  106.8 0.4 fusion.15
  107.2 2.7 fusion.4
  109.9 115.6 %psum.14 = f32[56,20]{0,1:T(8,128)S(1)} all-reduce(f32[56,20]{0,1:T(8,128)S(1)} %fusion.4), channel_id=1, replica_groups=mesh['gx'=8,'gy'=16,'gz'=4] {'gx','gy','gz'}, use_global_device_ids=true, to_apply=%region_0.0 | all-reduce | flops 1120 | bytes 8960 | tf_op jit(solution)/shard_map/psum | solution.py:66
  225.7 0.5 copy.17
  226.1 2.0 convolution_subtract_fusion
  228.1 0.9 fusion.58
  229.1 100.0 %psum.15 = f32[20,20]{0,1:T(8,128)S(1)} all-reduce(f32[20,20]{0,1:T(8,128)S(1)} %fusion.58), channel_id=1, replica_groups=mesh['gx'=8,'gy'=16,'gz'=4] {'gx','gy','gz'}, use_global_device_ids=true, to_apply=%region_1.0 | all-reduce | flops 400 | bytes 3200 | tf_op jit(solution)/shard_map/psum | solution.py:73
  329.2 1.8 cholesky.16
  331.0 0.6 compare_reduce_fusion
  331.7 0.7 fusion.48
  332.3 0.7 copy.10
  333.0 1.5 custom-call.6
  334.6 0.2 copy.19
  334.8 1.1 fusion.8
  335.9 1.0 copy.9
  (27 shorter events, 1.0 us)
Async XLA Ops:
  0.6 47.7 %copy-start.1 = (f32[4,8,8,128]{3,2,1,0:T(8,128)S(1)}, f32[4,8,8,128]{3,2,1,0:T(8,128)}, u32[]{:S(2)}) copy-start(f32[4,8,8,128]{3,2,1,0:T(8,128)} %param.4) | copy-start | bytes 393220
  1.8 10.7 %collective-permute-start.1 = (f32[4,8,8,1]{3,2,1,0:T(8,128)S(1)}, f32[4,8,8,1]{3,2,1,0:T(8,128)S(1)}, u32[]{:S(2)}, u32[]{:S(2)}) collective-permute-start(f32[4,8,8,1]{3,2,1,0:T(8,128)S(1)} %get-tuple-element.32), channel_id=1, source_target_pairs={{64,0},{128,64},{192,128},{256,192},{320,256},{384,320},{448,384},... | collective-permute-start | bytes 3080 | tf_op jit(solution)/shard_map/ppermute | solution.py:19
  10.6 3.9 %collective-permute-start = (f32[4,8,8,1]{3,2,1,0:T(8,128)S(1)}, f32[4,8,8,1]{3,2,1,0:T(8,128)S(1)}, u32[]{:S(2)}, u32[]{:S(2)}) collective-permute-start(f32[4,8,8,1]{3,2,1,0:T(8,128)S(1)} %get-tuple-element.33), channel_id=1, source_target_pairs={{0,64},{64,128},{128,192},{192,256},{256,320},{320,384},{384,448},... | collective-permute-start | bytes 3080 | tf_op jit(solution)/shard_map/ppermute | solution.py:16
  15.7 5.3 %collective-permute-start.3 = (f32[4,8,1,130]{3,2,1,0:T(1,128)S(1)}, f32[4,8,1,130]{3,2,1,0:T(1,128)S(1)}, u32[]{:S(2)}, u32[]{:S(2)}) collective-permute-start(f32[4,8,1,130]{3,2,1,0:T(1,128)S(1)} %get-tuple-element.24), channel_id=1, source_target_pairs={{4,0},{8,4},{12,8},{16,12},{20,16},{24,20},{28,24},{32,28},{36,32}... | collective-permute-start | bytes 49928 | tf_op jit(solution)/shard_map/ppermute | solution.py:19
  17.0 5.0 %collective-permute-start.2 = (f32[4,8,1,130]{3,2,1,0:T(1,128)S(1)}, f32[4,8,1,130]{3,2,1,0:T(1,128)S(1)}, u32[]{:S(2)}, u32[]{:S(2)}) collective-permute-start(f32[4,8,1,130]{3,2,1,0:T(1,128)S(1)} %get-tuple-element.25), channel_id=1, source_target_pairs={{0,4},{4,8},{8,12},{12,16},{16,20},{20,24},{24,28},{28,32},{32,36}... | collective-permute-start | bytes 49928 | tf_op jit(solution)/shard_map/ppermute | solution.py:16
  22.8 6.1 %collective-permute-start.4 = (f32[4,1,10,130]{3,2,1,0:T(8,128)S(1)}, f32[4,1,10,130]{3,2,1,0:T(8,128)S(1)}, u32[]{:S(2)}, u32[]{:S(2)}) collective-permute-start(f32[4,1,10,130]{3,2,1,0:T(8,128)S(1)} %get-tuple-element.16), channel_id=1, source_target_pairs={{1,0},{2,1},{3,2},{5,4},{6,5},{7,6},{9,8},{10,9},{11,10},{13,12},{... | collective-permute-start | bytes 62408 | tf_op jit(solution)/shard_map/ppermute | solution.py:19
  24.1 5.3 %collective-permute-start.5 = (f32[4,1,10,130]{3,2,1,0:T(8,128)S(1)}, f32[4,1,10,130]{3,2,1,0:T(8,128)S(1)}, u32[]{:S(2)}, u32[]{:S(2)}) collective-permute-start(f32[4,1,10,130]{3,2,1,0:T(8,128)S(1)} %get-tuple-element.17), channel_id=1, source_target_pairs={{0,1},{1,2},{2,3},{4,5},{5,6},{6,7},{8,9},{9,10},{10,11},{12,13},{... | collective-permute-start | bytes 62408 | tf_op jit(solution)/shard_map/ppermute | solution.py:16
  31.7 9.3 %collective-permute-start.7 = (f32[4,8,8,1]{3,2,1,0:T(8,128)S(1)}, f32[4,8,8,1]{3,2,1,0:T(8,128)S(1)}, u32[]{:S(2)}, u32[]{:S(2)}) collective-permute-start(f32[4,8,8,1]{3,2,1,0:T(8,128)S(1)} %get-tuple-element.30), channel_id=1, source_target_pairs={{64,0},{128,64},{192,128},{256,192},{320,256},{384,320},{448,384},... | collective-permute-start | bytes 3080 | tf_op jit(solution)/shard_map/ppermute | solution.py:19
  35.4 6.8 %collective-permute-start.6 = (f32[4,8,8,1]{3,2,1,0:T(8,128)S(1)}, f32[4,8,8,1]{3,2,1,0:T(8,128)S(1)}, u32[]{:S(2)}, u32[]{:S(2)}) collective-permute-start(f32[4,8,8,1]{3,2,1,0:T(8,128)S(1)} %get-tuple-element.31), channel_id=1, source_target_pairs={{0,64},{64,128},{128,192},{192,256},{256,320},{320,384},{384,448},... | collective-permute-start | bytes 3080 | tf_op jit(solution)/shard_map/ppermute | solution.py:16
  42.4 5.9 %collective-permute-start.9 = (f32[4,8,1,130]{3,2,1,0:T(1,128)S(1)}, f32[4,8,1,130]{3,2,1,0:T(1,128)S(1)}, u32[]{:S(2)}, u32[]{:S(2)}) collective-permute-start(f32[4,8,1,130]{3,2,1,0:T(1,128)S(1)} %get-tuple-element.22), channel_id=1, source_target_pairs={{4,0},{8,4},{12,8},{16,12},{20,16},{24,20},{28,24},{32,28},{36,32}... | collective-permute-start | bytes 49928 | tf_op jit(solution)/shard_map/ppermute | solution.py:19
  43.7 5.6 %collective-permute-start.8 = (f32[4,8,1,130]{3,2,1,0:T(1,128)S(1)}, f32[4,8,1,130]{3,2,1,0:T(1,128)S(1)}, u32[]{:S(2)}, u32[]{:S(2)}) collective-permute-start(f32[4,8,1,130]{3,2,1,0:T(1,128)S(1)} %get-tuple-element.23), channel_id=1, source_target_pairs={{0,4},{4,8},{8,12},{12,16},{16,20},{20,24},{24,28},{28,32},{32,36}... | collective-permute-start | bytes 49928 | tf_op jit(solution)/shard_map/ppermute | solution.py:16
  49.4 5.9 %collective-permute-start.10 = (f32[4,1,10,130]{3,2,1,0:T(8,128)S(1)}, f32[4,1,10,130]{3,2,1,0:T(8,128)S(1)}, u32[]{:S(2)}, u32[]{:S(2)}) collective-permute-start(f32[4,1,10,130]{3,2,1,0:T(8,128)S(1)} %get-tuple-element.14), channel_id=1, source_target_pairs={{1,0},{2,1},{3,2},{5,4},{6,5},{7,6},{9,8},{10,9},{11,10},{13,12},{... | collective-permute-start | bytes 62408 | tf_op jit(solution)/shard_map/ppermute | solution.py:19
  50.7 5.9 %collective-permute-start.11 = (f32[4,1,10,130]{3,2,1,0:T(8,128)S(1)}, f32[4,1,10,130]{3,2,1,0:T(8,128)S(1)}, u32[]{:S(2)}, u32[]{:S(2)}) collective-permute-start(f32[4,1,10,130]{3,2,1,0:T(8,128)S(1)} %get-tuple-element.15), channel_id=1, source_target_pairs={{0,1},{1,2},{2,3},{4,5},{5,6},{6,7},{8,9},{9,10},{10,11},{12,13},{... | collective-permute-start | bytes 62408 | tf_op jit(solution)/shard_map/ppermute | solution.py:16
  57.2 8.7 %collective-permute-start.13 = (f32[4,8,8,1]{3,2,1,0:T(8,128)S(1)}, f32[4,8,8,1]{3,2,1,0:T(8,128)S(1)}, u32[]{:S(2)}, u32[]{:S(2)}) collective-permute-start(f32[4,8,8,1]{3,2,1,0:T(8,128)S(1)} %get-tuple-element.28), channel_id=1, source_target_pairs={{64,0},{128,64},{192,128},{256,192},{320,256},{384,320},{448,384},... | collective-permute-start | bytes 3080 | tf_op jit(solution)/shard_map/ppermute | solution.py:19
  59.1 8.0 %collective-permute-start.12 = (f32[4,8,8,1]{3,2,1,0:T(8,128)S(1)}, f32[4,8,8,1]{3,2,1,0:T(8,128)S(1)}, u32[]{:S(2)}, u32[]{:S(2)}) collective-permute-start(f32[4,8,8,1]{3,2,1,0:T(8,128)S(1)} %get-tuple-element.29), channel_id=1, source_target_pairs={{0,64},{64,128},{128,192},{192,256},{256,320},{320,384},{384,448},... | collective-permute-start | bytes 3080 | tf_op jit(solution)/shard_map/ppermute | solution.py:16
  67.4 5.9 %collective-permute-start.15 = (f32[4,8,1,130]{3,2,1,0:T(1,128)S(1)}, f32[4,8,1,130]{3,2,1,0:T(1,128)S(1)}, u32[]{:S(2)}, u32[]{:S(2)}) collective-permute-start(f32[4,8,1,130]{3,2,1,0:T(1,128)S(1)} %get-tuple-element.20), channel_id=1, source_target_pairs={{4,0},{8,4},{12,8},{16,12},{20,16},{24,20},{28,24},{32,28},{36,32}... | collective-permute-start | bytes 49928 | tf_op jit(solution)/shard_map/ppermute | solution.py:19
  68.7 5.6 %collective-permute-start.14 = (f32[4,8,1,130]{3,2,1,0:T(1,128)S(1)}, f32[4,8,1,130]{3,2,1,0:T(1,128)S(1)}, u32[]{:S(2)}, u32[]{:S(2)}) collective-permute-start(f32[4,8,1,130]{3,2,1,0:T(1,128)S(1)} %get-tuple-element.21), channel_id=1, source_target_pairs={{0,4},{4,8},{8,12},{12,16},{16,20},{20,24},{24,28},{28,32},{32,36}... | collective-permute-start | bytes 49928 | tf_op jit(solution)/shard_map/ppermute | solution.py:16
  74.4 32.8 %copy-start = (f32[56,8,8,128]{3,2,1,0:T(8,128)S(1)}, f32[56,8,8,128]{3,2,1,0:T(8,128)}, u32[]{:S(2)}) copy-start(f32[56,8,8,128]{3,2,1,0:T(8,128)} %param.3) | copy-start | bytes 5505028
  74.4 6.1 %collective-permute-start.16 = (f32[4,1,10,130]{3,2,1,0:T(8,128)S(1)}, f32[4,1,10,130]{3,2,1,0:T(8,128)S(1)}, u32[]{:S(2)}, u32[]{:S(2)}) collective-permute-start(f32[4,1,10,130]{3,2,1,0:T(8,128)S(1)} %get-tuple-element.12), channel_id=1, source_target_pairs={{1,0},{2,1},{3,2},{5,4},{6,5},{7,6},{9,8},{10,9},{11,10},{13,12},{... | collective-permute-start | bytes 62408 | tf_op jit(solution)/shard_map/ppermute | solution.py:19
  75.8 5.9 %collective-permute-start.17 = (f32[4,1,10,130]{3,2,1,0:T(8,128)S(1)}, f32[4,1,10,130]{3,2,1,0:T(8,128)S(1)}, u32[]{:S(2)}, u32[]{:S(2)}) collective-permute-start(f32[4,1,10,130]{3,2,1,0:T(8,128)S(1)} %get-tuple-element.13), channel_id=1, source_target_pairs={{0,1},{1,2},{2,3},{4,5},{5,6},{6,7},{8,9},{9,10},{10,11},{12,13},{... | collective-permute-start | bytes 62408 | tf_op jit(solution)/shard_map/ppermute | solution.py:16
  82.3 8.7 %collective-permute-start.19 = (f32[4,8,8,1]{3,2,1,0:T(8,128)S(1)}, f32[4,8,8,1]{3,2,1,0:T(8,128)S(1)}, u32[]{:S(2)}, u32[]{:S(2)}) collective-permute-start(f32[4,8,8,1]{3,2,1,0:T(8,128)S(1)} %get-tuple-element.26), channel_id=1, source_target_pairs={{64,0},{128,64},{192,128},{256,192},{320,256},{384,320},{448,384},... | collective-permute-start | bytes 3080 | tf_op jit(solution)/shard_map/ppermute | solution.py:19
  84.3 8.0 %collective-permute-start.18 = (f32[4,8,8,1]{3,2,1,0:T(8,128)S(1)}, f32[4,8,8,1]{3,2,1,0:T(8,128)S(1)}, u32[]{:S(2)}, u32[]{:S(2)}) collective-permute-start(f32[4,8,8,1]{3,2,1,0:T(8,128)S(1)} %get-tuple-element.27), channel_id=1, source_target_pairs={{0,64},{64,128},{128,192},{192,256},{256,320},{320,384},{384,448},... | collective-permute-start | bytes 3080 | tf_op jit(solution)/shard_map/ppermute | solution.py:16
  92.5 5.9 %collective-permute-start.21 = (f32[4,8,1,130]{3,2,1,0:T(1,128)S(1)}, f32[4,8,1,130]{3,2,1,0:T(1,128)S(1)}, u32[]{:S(2)}, u32[]{:S(2)}) collective-permute-start(f32[4,8,1,130]{3,2,1,0:T(1,128)S(1)} %get-tuple-element.18), channel_id=1, source_target_pairs={{4,0},{8,4},{12,8},{16,12},{20,16},{24,20},{28,24},{32,28},{36,32}... | collective-permute-start | bytes 49928 | tf_op jit(solution)/shard_map/ppermute | solution.py:19
  93.8 5.6 %collective-permute-start.20 = (f32[4,8,1,130]{3,2,1,0:T(1,128)S(1)}, f32[4,8,1,130]{3,2,1,0:T(1,128)S(1)}, u32[]{:S(2)}, u32[]{:S(2)}) collective-permute-start(f32[4,8,1,130]{3,2,1,0:T(1,128)S(1)} %get-tuple-element.19), channel_id=1, source_target_pairs={{0,4},{4,8},{8,12},{12,16},{16,20},{20,24},{24,28},{28,32},{32,36}... | collective-permute-start | bytes 49928 | tf_op jit(solution)/shard_map/ppermute | solution.py:16
  99.5 5.9 %collective-permute-start.22 = (f32[4,1,10,130]{3,2,1,0:T(8,128)S(1)}, f32[4,1,10,130]{3,2,1,0:T(8,128)S(1)}, u32[]{:S(2)}, u32[]{:S(2)}) collective-permute-start(f32[4,1,10,130]{3,2,1,0:T(8,128)S(1)} %get-tuple-element.10), channel_id=1, source_target_pairs={{1,0},{2,1},{3,2},{5,4},{6,5},{7,6},{9,8},{10,9},{11,10},{13,12},{... | collective-permute-start | bytes 62408 | tf_op jit(solution)/shard_map/ppermute | solution.py:19
  100.8 5.9 %collective-permute-start.23 = (f32[4,1,10,130]{3,2,1,0:T(8,128)S(1)}, f32[4,1,10,130]{3,2,1,0:T(8,128)S(1)}, u32[]{:S(2)}, u32[]{:S(2)}) collective-permute-start(f32[4,1,10,130]{3,2,1,0:T(8,128)S(1)} %get-tuple-element.11), channel_id=1, source_target_pairs={{0,1},{1,2},{2,3},{4,5},{5,6},{6,7},{8,9},{9,10},{10,11},{12,13},{... | collective-permute-start | bytes 62408 | tf_op jit(solution)/shard_map/ppermute | solution.py:16
where the time goes:
time: 338 us; the launch traced here: 337 us
  blocking collectives  216 us (64%)
  starting transfers between devices  81.2 us (24%)
  waiting for transfers between devices  16.1 us (5%)
  other arithmetic  12.1 us (4%)
  matrix products  6.77 us (2%)
  local copies, waits for them, and re-layouts  3.91 us (1%)
    psum x1, blocking collectives, on_device(): coef = lax.psum(local_coef, ('gx', 'gy', 'gz')) / cell_total  116 us
    psum x1, blocking collectives, on_device(): gram = lax.psum(local_gram, ('gx', 'gy', 'gz')) / cell_total  100 us
    ppermute x12, starting transfers between devices, with_halo(): lax.ppermute(lax.slice_in_dim(block, block.shape[dim] - width, None, axis...  54.4 us
    ppermute x12, starting transfers between devices, with_halo(): lax.ppermute(lax.slice_in_dim(block, 0, width, axis=dim), axis, backward)  26.8 us
    ppermute x12, waiting for transfers between devices, with_halo(): lax.ppermute(lax.slice_in_dim(block, block.shape[dim] - width, None, axis...  13.9 us
  transfers between devices with their start and end apart: 24, of which 15 were waited for; matrix products, arithmetic and copies ran while one was open for 0% of the time, Pallas kernels for 0%

commit v1 on v0

--- a/solution.py
+++ b/solution.py
@@ -70,7 +70,7 @@
     local_gram = jnp.dot(
         projected, projected.T, precision=highest, preferred_element_type=jnp.float32
     )
-    gram = lax.psum(local_gram, ("gx", "gy", "gz")) / cell_total
+    gram = lax.psum(lax.psum(local_gram, "gx"), ("gy", "gz")) / cell_total
     lower = jnp.linalg.cholesky(gram)
     solved = lax.linalg.triangular_solve(lower, projected, left_side=True, lower=True)
     return (solved.reshape(basis.shape), lower.T)

time: 338 us -> 535 us (1.58)
  the two profiles are of different devices: /device:TPU:1 before, /device:TPU:8 now
where the time goes in v1:
time: 535 us; the launch traced here: 534 us
  blocking collectives  412 us (77%)
  starting transfers between devices  66.1 us (12%)
  waiting for transfers between devices  32.7 us (6%)
  other arithmetic  12.1 us (2%)
  matrix products  6.77 us (1%)
    psum x2, blocking collectives, on_device(): gram = lax.psum(lax.psum(local_gram, 'gx'), ('gy', 'gz')) / cell_total  298 us
    psum x1, blocking collectives, on_device(): coef = lax.psum(local_coef, ('gx', 'gy', 'gz')) / cell_total  113 us
    ppermute x12, starting transfers between devices, with_halo(): lax.ppermute(lax.slice_in_dim(block, block.shape[dim] - width, None, axis...  48 us
    ppermute x12, waiting for transfers between devices, with_halo(): lax.ppermute(lax.slice_in_dim(block, block.shape[dim] - width, None, axis...  31.4 us
    ppermute x12, starting transfers between devices, with_halo(): lax.ppermute(lax.slice_in_dim(block, 0, width, axis=dim), axis, backward)  18.2 us
  transfers between devices with their start and end apart: 24, of which 19 were waited for; matrix products, arithmetic and copies ran while one was open for 0% of the time, Pallas kernels for 0%

profile of v1, /device:TPU:8, one launch (start us, length us, event | category | flops | bytes accessed | tf_op | source)
XLA Modules:
  0.0 534.3 jit_solution(10770106594382494217)
XLA Ops:
  0.6 1.1 fusion.57
  1.8 1.9 collective-permute-start.1
  3.7 2.4 collective-permute-start
  6.2 8.0 %collective-permute-done = f32[4,8,8,1]{3,2,1,0:T(8,128)S(1)} collective-permute-done((f32[4,8,8,1]{3,2,1,0:T(8,128)S(1)}, f32[4,8,8,1]{3,2,1,0:T(8,128)S(1)}, u32[]{:S(2)}, u32[]{:S(2)}) %collective-permute-start) | collective-permute-done | bytes 1056 | tf_op jit(solution)/shard_map/ppermute | solution.py:16
  14.2 1.2 pad_maximum_fusion.101
  15.4 1.3 collective-permute-start.3
  16.7 4.5 collective-permute-start.2
  21.3 1.6 collective-permute-done.2
  22.9 0.9 pad_maximum_fusion.91
  23.7 1.3 collective-permute-start.4
  25.0 4.5 collective-permute-start.5
  29.6 0.8 broadcast_multiply_fusion.1
  30.4 1.1 collective-permute-done.5
  31.5 2.1 broadcast_multiply_fusion
  33.7 1.9 collective-permute-start.7
  35.6 2.4 collective-permute-start.6
  38.1 3.8 collective-permute-done.6
  41.9 0.3 pad_maximum_fusion.98
  42.2 1.3 collective-permute-start.9
  43.5 4.9 collective-permute-start.8
  48.4 1.5 collective-permute-done.8
  50.0 1.3 collective-permute-start.10
  51.3 4.9 collective-permute-start.11
  56.3 0.3 collective-permute-done.10
  56.5 1.6 collective-permute-done.11
  58.1 0.4 constant_dynamic-update-slice_fusion.1
  58.7 1.9 collective-permute-start.13
  60.6 2.4 collective-permute-start.12
  63.1 3.8 collective-permute-done.12
  66.9 0.3 pad_maximum_fusion.95
  67.2 1.3 collective-permute-start.15
  68.5 4.9 collective-permute-start.14
  73.3 1.6 collective-permute-done.14
  75.0 1.4 collective-permute-start.16
  76.5 4.9 collective-permute-start.17
  81.4 0.3 collective-permute-done.16
  81.7 1.6 collective-permute-done.17
  83.2 0.4 constant_dynamic-update-slice_fusion
  83.8 1.9 collective-permute-start.19
  85.7 2.4 collective-permute-start.18
  88.2 3.8 collective-permute-done.18
  92.0 0.3 pad_maximum_fusion.92
  92.3 1.3 collective-permute-start.21
  93.6 4.9 collective-permute-start.20
  98.4 1.6 collective-permute-done.20
  100.1 1.3 collective-permute-start.22
  101.4 4.9 collective-permute-start.23
  106.3 0.3 collective-permute-done.22
  106.6 1.6 collective-permute-done.23
  108.2 0.4 fusion.15
  108.7 2.7 fusion.4
  111.4 113.1 %psum.21 = f32[56,20]{0,1:T(8,128)S(1)} all-reduce(f32[56,20]{0,1:T(8,128)S(1)} %fusion.4), channel_id=1, replica_groups=mesh['gx'=8,'gy'=16,'gz'=4] {'gx','gy','gz'}, use_global_device_ids=true, to_apply=%region_0.0 | all-reduce | flops 1120 | bytes 8960 | tf_op jit(solution)/shard_map/psum | solution.py:66
  224.6 0.5 copy.17
  225.1 2.0 convolution_subtract_fusion
  227.1 0.9 fusion.58
  228.0 22.7 %psum.22 = f32[20,20]{0,1:T(8,128)S(1)} all-reduce(f32[20,20]{0,1:T(8,128)S(1)} %fusion.58), channel_id=1, replica_groups=mesh['gx'=8,'gy'=16,'gz'=4] {'gx'}, use_global_device_ids=true, to_apply=%region_1.0 | all-reduce | flops 400 | bytes 3200 | tf_op jit(solution)/shard_map/psum | solution.py:73
  250.7 275.8 %psum.23 = f32[20,20]{0,1:T(8,128)S(1)} all-reduce(f32[20,20]{0,1:T(8,128)S(1)} %psum.22), channel_id=1, replica_groups=mesh['gx'=8,'gy'=16,'gz'=4] {'gy','gz'}, use_global_device_ids=true, to_apply=%region_2.0 | all-reduce | flops 400 | bytes 3200 | tf_op jit(solution)/shard_map/psum | solution.py:73
  526.6 1.8 cholesky.16
  528.5 0.6 compare_reduce_fusion
  529.1 0.7 fusion.48
  529.8 0.7 copy.10
  530.4 1.5 custom-call.6
  532.2 1.1 fusion.8
  533.3 1.0 copy.9
  (28 shorter events, 1.5 us)
Async XLA Ops:
  0.6 47.7 %copy-start.1 = (f32[4,8,8,128]{3,2,1,0:T(8,128)S(1)}, f32[4,8,8,128]{3,2,1,0:T(8,128)}, u32[]{:S(2)}) copy-start(f32[4,8,8,128]{3,2,1,0:T(8,128)} %param.4) | copy-start | bytes 393220
  1.8 4.4 collective-permute-start.1
  3.7 10.5 %collective-permute-start = (f32[4,8,8,1]{3,2,1,0:T(8,128)S(1)}, f32[4,8,8,1]{3,2,1,0:T(8,128)S(1)}, u32[]{:S(2)}, u32[]{:S(2)}) collective-permute-start(f32[4,8,8,1]{3,2,1,0:T(8,128)S(1)} %get-tuple-element.33), channel_id=1, source_target_pairs={{0,64},{64,128},{128,192},{192,256},{256,320},{320,384},{384,448},... | collective-permute-start | bytes 3080 | tf_op jit(solution)/shard_map/ppermute | solution.py:16
  15.4 5.9 %collective-permute-start.3 = (f32[4,8,1,130]{3,2,1,0:T(1,128)S(1)}, f32[4,8,1,130]{3,2,1,0:T(1,128)S(1)}, u32[]{:S(2)}, u32[]{:S(2)}) collective-permute-start(f32[4,8,1,130]{3,2,1,0:T(1,128)S(1)} %get-tuple-element.24), channel_id=1, source_target_pairs={{4,0},{8,4},{12,8},{16,12},{20,16},{24,20},{28,24},{32,28},{36,32}... | collective-permute-start | bytes 49928 | tf_op jit(solution)/shard_map/ppermute | solution.py:19
  16.7 6.1 %collective-permute-start.2 = (f32[4,8,1,130]{3,2,1,0:T(1,128)S(1)}, f32[4,8,1,130]{3,2,1,0:T(1,128)S(1)}, u32[]{:S(2)}, u32[]{:S(2)}) collective-permute-start(f32[4,8,1,130]{3,2,1,0:T(1,128)S(1)} %get-tuple-element.25), channel_id=1, source_target_pairs={{0,4},{4,8},{8,12},{12,16},{16,20},{20,24},{24,28},{28,32},{32,36}... | collective-permute-start | bytes 49928 | tf_op jit(solution)/shard_map/ppermute | solution.py:16
  23.7 6.6 %collective-permute-start.4 = (f32[4,1,10,130]{3,2,1,0:T(8,128)S(1)}, f32[4,1,10,130]{3,2,1,0:T(8,128)S(1)}, u32[]{:S(2)}, u32[]{:S(2)}) collective-permute-start(f32[4,1,10,130]{3,2,1,0:T(8,128)S(1)} %get-tuple-element.16), channel_id=1, source_target_pairs={{1,0},{2,1},{3,2},{5,4},{6,5},{7,6},{9,8},{10,9},{11,10},{13,12},{... | collective-permute-start | bytes 62408 | tf_op jit(solution)/shard_map/ppermute | solution.py:19
  25.0 6.4 %collective-permute-start.5 = (f32[4,1,10,130]{3,2,1,0:T(8,128)S(1)}, f32[4,1,10,130]{3,2,1,0:T(8,128)S(1)}, u32[]{:S(2)}, u32[]{:S(2)}) collective-permute-start(f32[4,1,10,130]{3,2,1,0:T(8,128)S(1)} %get-tuple-element.17), channel_id=1, source_target_pairs={{0,1},{1,2},{2,3},{4,5},{5,6},{6,7},{8,9},{9,10},{10,11},{12,13},{... | collective-permute-start | bytes 62408 | tf_op jit(solution)/shard_map/ppermute | solution.py:16
  33.7 4.4 collective-permute-start.7
  35.6 6.3 %collective-permute-start.6 = (f32[4,8,8,1]{3,2,1,0:T(8,128)S(1)}, f32[4,8,8,1]{3,2,1,0:T(8,128)S(1)}, u32[]{:S(2)}, u32[]{:S(2)}) collective-permute-start(f32[4,8,8,1]{3,2,1,0:T(8,128)S(1)} %get-tuple-element.31), channel_id=1, source_target_pairs={{0,64},{64,128},{128,192},{192,256},{256,320},{320,384},{384,448},... | collective-permute-start | bytes 3080 | tf_op jit(solution)/shard_map/ppermute | solution.py:16
  42.2 6.2 %collective-permute-start.9 = (f32[4,8,1,130]{3,2,1,0:T(1,128)S(1)}, f32[4,8,1,130]{3,2,1,0:T(1,128)S(1)}, u32[]{:S(2)}, u32[]{:S(2)}) collective-permute-start(f32[4,8,1,130]{3,2,1,0:T(1,128)S(1)} %get-tuple-element.22), channel_id=1, source_target_pairs={{4,0},{8,4},{12,8},{16,12},{20,16},{24,20},{28,24},{32,28},{36,32}... | collective-permute-start | bytes 49928 | tf_op jit(solution)/shard_map/ppermute | solution.py:19
  43.5 6.4 %collective-permute-start.8 = (f32[4,8,1,130]{3,2,1,0:T(1,128)S(1)}, f32[4,8,1,130]{3,2,1,0:T(1,128)S(1)}, u32[]{:S(2)}, u32[]{:S(2)}) collective-permute-start(f32[4,8,1,130]{3,2,1,0:T(1,128)S(1)} %get-tuple-element.23), channel_id=1, source_target_pairs={{0,4},{4,8},{8,12},{12,16},{16,20},{20,24},{24,28},{28,32},{32,36}... | collective-permute-start | bytes 49928 | tf_op jit(solution)/shard_map/ppermute | solution.py:16
  50.0 6.5 %collective-permute-start.10 = (f32[4,1,10,130]{3,2,1,0:T(8,128)S(1)}, f32[4,1,10,130]{3,2,1,0:T(8,128)S(1)}, u32[]{:S(2)}, u32[]{:S(2)}) collective-permute-start(f32[4,1,10,130]{3,2,1,0:T(8,128)S(1)} %get-tuple-element.14), channel_id=1, source_target_pairs={{1,0},{2,1},{3,2},{5,4},{6,5},{7,6},{9,8},{10,9},{11,10},{13,12},{... | collective-permute-start | bytes 62408 | tf_op jit(solution)/shard_map/ppermute | solution.py:19
  51.3 6.8 %collective-permute-start.11 = (f32[4,1,10,130]{3,2,1,0:T(8,128)S(1)}, f32[4,1,10,130]{3,2,1,0:T(8,128)S(1)}, u32[]{:S(2)}, u32[]{:S(2)}) collective-permute-start(f32[4,1,10,130]{3,2,1,0:T(8,128)S(1)} %get-tuple-element.15), channel_id=1, source_target_pairs={{0,1},{1,2},{2,3},{4,5},{5,6},{6,7},{8,9},{9,10},{10,11},{12,13},{... | collective-permute-start | bytes 62408 | tf_op jit(solution)/shard_map/ppermute | solution.py:16
  58.7 4.4 collective-permute-start.13
  60.6 6.3 %collective-permute-start.12 = (f32[4,8,8,1]{3,2,1,0:T(8,128)S(1)}, f32[4,8,8,1]{3,2,1,0:T(8,128)S(1)}, u32[]{:S(2)}, u32[]{:S(2)}) collective-permute-start(f32[4,8,8,1]{3,2,1,0:T(8,128)S(1)} %get-tuple-element.29), channel_id=1, source_target_pairs={{0,64},{64,128},{128,192},{192,256},{256,320},{320,384},{384,448},... | collective-permute-start | bytes 3080 | tf_op jit(solution)/shard_map/ppermute | solution.py:16
  67.2 6.2 %collective-permute-start.15 = (f32[4,8,1,130]{3,2,1,0:T(1,128)S(1)}, f32[4,8,1,130]{3,2,1,0:T(1,128)S(1)}, u32[]{:S(2)}, u32[]{:S(2)}) collective-permute-start(f32[4,8,1,130]{3,2,1,0:T(1,128)S(1)} %get-tuple-element.20), channel_id=1, source_target_pairs={{4,0},{8,4},{12,8},{16,12},{20,16},{24,20},{28,24},{32,28},{36,32}... | collective-permute-start | bytes 49928 | tf_op jit(solution)/shard_map/ppermute | solution.py:19
  68.5 6.4 %collective-permute-start.14 = (f32[4,8,1,130]{3,2,1,0:T(1,128)S(1)}, f32[4,8,1,130]{3,2,1,0:T(1,128)S(1)}, u32[]{:S(2)}, u32[]{:S(2)}) collective-permute-start(f32[4,8,1,130]{3,2,1,0:T(1,128)S(1)} %get-tuple-element.21), channel_id=1, source_target_pairs={{0,4},{4,8},{8,12},{12,16},{16,20},{20,24},{24,28},{28,32},{32,36}... | collective-permute-start | bytes 49928 | tf_op jit(solution)/shard_map/ppermute | solution.py:16
  75.0 33.7 %copy-start = (f32[56,8,8,128]{3,2,1,0:T(8,128)S(1)}, f32[56,8,8,128]{3,2,1,0:T(8,128)}, u32[]{:S(2)}) copy-start(f32[56,8,8,128]{3,2,1,0:T(8,128)} %param.3) | copy-start | bytes 5505028
  75.0 6.6 %collective-permute-start.16 = (f32[4,1,10,130]{3,2,1,0:T(8,128)S(1)}, f32[4,1,10,130]{3,2,1,0:T(8,128)S(1)}, u32[]{:S(2)}, u32[]{:S(2)}) collective-permute-start(f32[4,1,10,130]{3,2,1,0:T(8,128)S(1)} %get-tuple-element.12), channel_id=1, source_target_pairs={{1,0},{2,1},{3,2},{5,4},{6,5},{7,6},{9,8},{10,9},{11,10},{13,12},{... | collective-permute-start | bytes 62408 | tf_op jit(solution)/shard_map/ppermute | solution.py:19
  76.5 6.8 %collective-permute-start.17 = (f32[4,1,10,130]{3,2,1,0:T(8,128)S(1)}, f32[4,1,10,130]{3,2,1,0:T(8,128)S(1)}, u32[]{:S(2)}, u32[]{:S(2)}) collective-permute-start(f32[4,1,10,130]{3,2,1,0:T(8,128)S(1)} %get-tuple-element.13), channel_id=1, source_target_pairs={{0,1},{1,2},{2,3},{4,5},{5,6},{6,7},{8,9},{9,10},{10,11},{12,13},{... | collective-permute-start | bytes 62408 | tf_op jit(solution)/shard_map/ppermute | solution.py:16
  83.8 4.4 collective-permute-start.19
  85.7 6.3 %collective-permute-start.18 = (f32[4,8,8,1]{3,2,1,0:T(8,128)S(1)}, f32[4,8,8,1]{3,2,1,0:T(8,128)S(1)}, u32[]{:S(2)}, u32[]{:S(2)}) collective-permute-start(f32[4,8,8,1]{3,2,1,0:T(8,128)S(1)} %get-tuple-element.27), channel_id=1, source_target_pairs={{0,64},{64,128},{128,192},{192,256},{256,320},{320,384},{384,448},... | collective-permute-start | bytes 3080 | tf_op jit(solution)/shard_map/ppermute | solution.py:16
  92.3 6.2 %collective-permute-start.21 = (f32[4,8,1,130]{3,2,1,0:T(1,128)S(1)}, f32[4,8,1,130]{3,2,1,0:T(1,128)S(1)}, u32[]{:S(2)}, u32[]{:S(2)}) collective-permute-start(f32[4,8,1,130]{3,2,1,0:T(1,128)S(1)} %get-tuple-element.18), channel_id=1, source_target_pairs={{4,0},{8,4},{12,8},{16,12},{20,16},{24,20},{28,24},{32,28},{36,32}... | collective-permute-start | bytes 49928 | tf_op jit(solution)/shard_map/ppermute | solution.py:19
  93.6 6.4 %collective-permute-start.20 = (f32[4,8,1,130]{3,2,1,0:T(1,128)S(1)}, f32[4,8,1,130]{3,2,1,0:T(1,128)S(1)}, u32[]{:S(2)}, u32[]{:S(2)}) collective-permute-start(f32[4,8,1,130]{3,2,1,0:T(1,128)S(1)} %get-tuple-element.19), channel_id=1, source_target_pairs={{0,4},{4,8},{8,12},{12,16},{16,20},{20,24},{24,28},{28,32},{32,36}... | collective-permute-start | bytes 49928 | tf_op jit(solution)/shard_map/ppermute | solution.py:16
  100.1 6.5 %collective-permute-start.22 = (f32[4,1,10,130]{3,2,1,0:T(8,128)S(1)}, f32[4,1,10,130]{3,2,1,0:T(8,128)S(1)}, u32[]{:S(2)}, u32[]{:S(2)}) collective-permute-start(f32[4,1,10,130]{3,2,1,0:T(8,128)S(1)} %get-tuple-element.10), channel_id=1, source_target_pairs={{1,0},{2,1},{3,2},{5,4},{6,5},{7,6},{9,8},{10,9},{11,10},{13,12},{... | collective-permute-start | bytes 62408 | tf_op jit(solution)/shard_map/ppermute | solution.py:19
  101.4 6.8 %collective-permute-start.23 = (f32[4,1,10,130]{3,2,1,0:T(8,128)S(1)}, f32[4,1,10,130]{3,2,1,0:T(8,128)S(1)}, u32[]{:S(2)}, u32[]{:S(2)}) collective-permute-start(f32[4,1,10,130]{3,2,1,0:T(8,128)S(1)} %get-tuple-element.11), channel_id=1, source_target_pairs={{0,1},{1,2},{2,3},{4,5},{5,6},{6,7},{8,9},{9,10},{10,11},{12,13},{... | collective-permute-start | bytes 62408 | tf_op jit(solution)/shard_map/ppermute | solution.py:16
